TPU v7x, 32 devices: a whole 2x2x4 slice. The times are simulated.
32 devices in a mesh: dp: 8 (over z, y), mp: 4 (over x, core).
Axes of the slice: x: 2, y: 2, z: 4, core: 2. Of those that a mesh axis runs over, the one named last changes fastest.
Arguments:
- tokens: bfloat16 [16384, 768], P('dp'), may hold values from -6 to 6
- lengths: int32 [8, 2], P('dp'), may hold values from 0 to 2048, as said below
- mix_gain: float32 [768], replicated, may hold values from 0.5 to 1.5
- mix_shift: float32 [768], replicated, may hold values from -4 to 4
- proj_in: bfloat16 [768, 3, 768], P(None, None, 'mp'), may hold values from -0.21875 to 0.21875
- bias_in: float32 [3, 768], P(None, 'mp'), may hold values from -4 to 4
- short_taps: float32 [3, 3, 768], P(None, None, 'mp'), may hold values from -6 to 6
- long_taps: bfloat16 [2048, 768], P('dp', 'mp'), may hold values from -0.75 to 0.75
- decay_rates: float32 [768], P('mp'), may hold values from 0.00024414062 to 0.05
- skip_gain: float32 [768], P('mp'), may hold values from -6 to 6
- proj_out: bfloat16 [768, 768], P('mp'), may hold values from -0.21875 to 0.21875
- bias_out: float32 [768], replicated, may hold values from -4 to 4
- mlp_gain: float32 [768], replicated, may hold values from 0.5 to 1.5
- mlp_shift: float32 [768], replicated, may hold values from -4 to 4
- proj_up: bfloat16 [768, 3072], P(None, 'mp'), may hold values from -0.21875 to 0.21875
- bias_up: float32 [3072], P('mp'), may hold values from -4 to 4
- proj_down: bfloat16 [3072, 768], P('mp'), may hold values from -0.109375 to 0.109375
- bias_down: float32 [768], replicated, may hold values from -4 to 4
- cotangent: bfloat16 [16384, 768], P('dp'), may hold values from -6 to 6
Outputs:
- output: bfloat16 [16384, 768], P('dp')
- input_grad: float32 [16384, 768], P('dp')
- grad_mix_gain: float32 [768], replicated
- grad_mix_shift: float32 [768], replicated
- grad_proj_in: float32 [768, 3, 768], P(None, None, 'mp')
- grad_bias_in: float32 [3, 768], P(None, 'mp')
- grad_short_taps: float32 [3, 3, 768], P(None, None, 'mp')
- grad_long_taps: float32 [2048, 768], P('dp', 'mp')
- grad_decay_rates: float32 [768], P('mp')
- grad_skip_gain: float32 [768], P('mp')
- grad_proj_out: float32 [768, 768], P('mp')
- grad_bias_out: float32 [768], replicated
- grad_mlp_gain: float32 [768], replicated
- grad_mlp_shift: float32 [768], replicated
- grad_proj_up: float32 [768, 3072], P(None, 'mp')
- grad_bias_up: float32 [3072], P('mp')
- grad_proj_down: float32 [3072, 768], P('mp')
- grad_bias_down: float32 [768], replicated
Inputs may be any that keep to these rules, and one draw needn't show every extreme that they name: Row g gives the lengths of the documents packed in order into group g's 2048 tokens: either one document of 2048 tokens and 0, or two of half of 2048 each; exactly half of the rows hold two documents.
All inputs are finite; a program needn't handle non-finite values.
Results may differ from a plain program's by a relative error of at most 0.024.
Values may be sent and summed in bfloat16 or wider, within the bound.
No kernel may reach another device: no remote copies, remote signals or barrier semaphores. Data moves between devices by JAX's collectives and lax.ppermute only.
A program may use at most 256 MiB of HBM per device.

v0:
```python
from functools import partial
import math
import jax
import jax.numpy as jnp
from jax import lax
from jax.sharding import PartitionSpec as P


def layer_norm(values, scale_vec, shift_vec):
    average = jnp.mean(values, axis=-1, keepdims=True)
    centered = values - average
    variance = jnp.mean(centered * centered, axis=-1, keepdims=True)
    return centered * lax.rsqrt(variance + 1e-05) * scale_vec + shift_vec


def short_mix(first_len, streams, short_taps):
    seq_len = streams.shape[0]
    positions = jnp.arange(seq_len, dtype=jnp.int32)[:, None, None]
    result = short_taps[0] * streams
    for offset in (1, 2):
        shifted = jnp.concatenate(
            [jnp.zeros((offset,) + streams.shape[1:], streams.dtype), streams[:-offset]], axis=0
        )
        valid_mask = (positions >= offset) & (
            (positions < first_len) | (positions - offset >= first_len)
        )
        result = result + valid_mask.astype(streams.dtype) * (short_taps[offset] * shifted)
    return (result[:, 0], result[:, 1] * result[:, 2])


def build_kernel(raw_taps, decay_rates):
    seq_len = raw_taps.shape[0]
    positions = jnp.arange(seq_len).astype(raw_taps.dtype)[:, None]
    decayed = raw_taps * jnp.exp(-decay_rates * positions)
    padded = jnp.pad(decayed, ((1, 1), (0, 0)))
    pooled = (padded[:-2] + padded[1:-1] + padded[2:]) / 3.0
    return jnp.sign(pooled) * jnp.maximum(jnp.abs(pooled) - 0.003, 0.0)


def gate_mix(queries, conv_out, mixed_in, skip_gain):
    return queries * (conv_out + skip_gain * mixed_in)


def gelu_exact(values):
    return jax.nn.gelu(values, approximate=False)


def plain_product(lhs_mat, rhs_mat):
    return jnp.dot(lhs_mat, rhs_mat, preferred_element_type=jnp.float32)


def tall_product(lhs_mat, rhs_mat):
    return lax.dot_general(
        lhs_mat, rhs_mat, (((0,), (0,)), ((), ())), preferred_element_type=jnp.float32
    )


def wide_product(lhs_mat, rhs_mat):
    return lax.dot_general(
        lhs_mat, rhs_mat, (((1,), (1,)), ((), ())), preferred_element_type=jnp.float32
    )


def exact_product(lhs_mat, rhs_mat):
    return jnp.dot(
        lhs_mat, rhs_mat, precision=lax.Precision.HIGHEST, preferred_element_type=jnp.float32
    )


def across(table, values):
    return jnp.einsum(
        "jn,knc->kjc",
        table,
        values,
        precision=lax.Precision.HIGHEST,
        preferred_element_type=jnp.float32,
    )


def dft_pair(out_count, in_count, period):
    outer = lax.iota(jnp.int32, out_count)[:, None]
    inner = lax.iota(jnp.int32, in_count)[None, :]
    angles = (outer * inner % period).astype(jnp.float32) * (2.0 * math.pi / period)
    return (jnp.cos(angles), jnp.sin(angles))


def twiddles(rows_p, cols_q, period):
    outer = lax.iota(jnp.int32, rows_p)[:, None]
    inner = lax.iota(jnp.int32, cols_q)[None, :]
    angles = (outer * inner % period).astype(jnp.float32) * (2.0 * math.pi / period)
    return (jnp.cos(angles)[:, :, None], jnp.sin(angles)[:, :, None])


def split_sizes(seq_len):
    period = 2 * seq_len
    exponent = period.bit_length() - 1
    rows_p = 2 ** ((exponent + 1) // 2)
    return (period, rows_p, period // rows_p)


def spectrum(signal):
    seq_len, columns = signal.shape
    period, rows_p, cols_q = split_sizes(seq_len)
    half = rows_p // 2
    flat = signal.reshape(half, cols_q * columns)
    cos_p, sin_p = dft_pair(rows_p, half, rows_p)
    first_re = exact_product(cos_p, flat).reshape(rows_p, cols_q, columns)
    first_im = -exact_product(sin_p, flat).reshape(rows_p, cols_q, columns)
    turn_cos, turn_sin = twiddles(rows_p, cols_q, period)
    turned_re = first_re * turn_cos + first_im * turn_sin
    turned_im = first_im * turn_cos - first_re * turn_sin
    cos_q, sin_q = dft_pair(cols_q, cols_q, cols_q)
    spec_re = across(cos_q, turned_re) + across(sin_q, turned_im)
    spec_im = across(cos_q, turned_im) - across(sin_q, turned_re)
    return (spec_re, spec_im)


def inverse_real(spec_re, spec_im):
    rows_p, cols_q, columns = spec_re.shape
    period = rows_p * cols_q
    half = rows_p // 2
    cos_q, sin_q = dft_pair(cols_q, cols_q, cols_q)
    back_re = across(cos_q, spec_re) - across(sin_q, spec_im)
    back_im = across(cos_q, spec_im) + across(sin_q, spec_re)
    turn_cos, turn_sin = twiddles(rows_p, cols_q, period)
    turned_re = back_re * turn_cos - back_im * turn_sin
    turned_im = back_im * turn_cos + back_re * turn_sin
    cos_i, sin_i = dft_pair(half, rows_p, rows_p)
    result = exact_product(cos_i, turned_re.reshape(rows_p, cols_q * columns)) - exact_product(
        sin_i, turned_im.reshape(rows_p, cols_q * columns)
    )
    return result.reshape(half * cols_q, columns) / float(period)


def long_conv(mixed_in, kernel, mask_one, mask_two):
    channels = mixed_in.shape[1]
    stacked = jnp.concatenate([mask_one * mixed_in, mask_two * mixed_in, kernel], axis=1)
    spec_re, spec_im = spectrum(stacked)
    sig_re = spec_re[:, :, : 2 * channels]
    sig_im = spec_im[:, :, : 2 * channels]
    ker_re = jnp.tile(spec_re[:, :, 2 * channels :], (1, 1, 2))
    ker_im = jnp.tile(spec_im[:, :, 2 * channels :], (1, 1, 2))
    prod_re = sig_re * ker_re - sig_im * ker_im
    prod_im = sig_re * ker_im + sig_im * ker_re
    totals = inverse_real(prod_re, prod_im)
    return mask_one * totals[:, :channels] + mask_two * totals[:, channels:]


def long_conv_back(grad_conv, mixed_in, kernel, mask_one, mask_two):
    channels = mixed_in.shape[1]
    stacked = jnp.concatenate(
        [
            mask_one * mixed_in,
            mask_two * mixed_in,
            mask_one * grad_conv,
            mask_two * grad_conv,
            kernel,
        ],
        axis=1,
    )
    spec_re, spec_im = spectrum(stacked)
    sig_re = spec_re[:, :, : 2 * channels]
    sig_im = spec_im[:, :, : 2 * channels]
    out_re = spec_re[:, :, 2 * channels : 4 * channels]
    out_im = spec_im[:, :, 2 * channels : 4 * channels]
    ker_re = jnp.tile(spec_re[:, :, 4 * channels :], (1, 1, 2))
    ker_im = jnp.tile(spec_im[:, :, 4 * channels :], (1, 1, 2))
    back_in_re = ker_re * out_re + ker_im * out_im
    back_in_im = ker_re * out_im - ker_im * out_re
    cor_re = sig_re * out_re + sig_im * out_im
    cor_im = sig_re * out_im - sig_im * out_re
    cor_re = cor_re[:, :, :channels] + cor_re[:, :, channels:]
    cor_im = cor_im[:, :, :channels] + cor_im[:, :, channels:]
    totals = inverse_real(
        jnp.concatenate([back_in_re, cor_re], axis=2), jnp.concatenate([back_in_im, cor_im], axis=2)
    )
    grad_mixed = mask_one * totals[:, :channels] + mask_two * totals[:, channels : 2 * channels]
    return (grad_mixed, totals[:, 2 * channels :])


def per_device(
    tokens,
    lengths,
    mix_gain,
    mix_shift,
    proj_in,
    bias_in,
    short_taps,
    long_taps,
    decay_rates,
    skip_gain,
    proj_out,
    bias_out,
    mlp_gain,
    mlp_shift,
    proj_up,
    bias_up,
    proj_down,
    bias_down,
    cotangent,
):
    seq_len, width = tokens.shape
    channels = proj_in.shape[2]
    first_len = lengths[0, 0]
    second_len = lengths[0, 1]
    positions = jnp.arange(seq_len, dtype=jnp.int32)[:, None]
    mask_one = (positions < first_len).astype(jnp.float32)
    mask_two = ((positions >= first_len) & (positions < first_len + second_len)).astype(jnp.float32)
    tokens_f = tokens.astype(jnp.float32)
    normed, norm_pull = jax.vjp(layer_norm, tokens_f, mix_gain, mix_shift)
    normed_low = normed.astype(jnp.bfloat16)
    proj_flat = proj_in.reshape(width, 3 * channels)
    streams = (plain_product(normed_low, proj_flat) + bias_in.reshape(-1)).reshape(
        seq_len, 3, channels
    )
    (queries, mixed_in), short_pull = jax.vjp(partial(short_mix, first_len), streams, short_taps)
    gathered = lax.all_gather(long_taps, "dp", axis=0, tiled=True)
    kernel, kernel_pull = jax.vjp(build_kernel, gathered.astype(jnp.float32), decay_rates)
    conv_out = long_conv(mixed_in, kernel, mask_one, mask_two)
    gated_out, gate_pull = jax.vjp(gate_mix, queries, conv_out, mixed_in, skip_gain)
    gated_low = gated_out.astype(jnp.bfloat16)
    attn_terms = plain_product(gated_low, proj_out)
    attn_out = lax.psum(attn_terms.astype(jnp.bfloat16), "mp").astype(jnp.float32) + bias_out
    hidden_one = tokens_f + attn_out
    normed_two, norm_two_pull = jax.vjp(layer_norm, hidden_one, mlp_gain, mlp_shift)
    normed_two_low = normed_two.astype(jnp.bfloat16)
    pre_act = plain_product(normed_two_low, proj_up) + bias_up
    hidden, gelu_pull = jax.vjp(gelu_exact, pre_act)
    hidden_low = hidden.astype(jnp.bfloat16)
    down_terms = plain_product(hidden_low, proj_down)
    mlp_out = lax.psum(down_terms.astype(jnp.bfloat16), "mp").astype(jnp.float32) + bias_down
    output = (hidden_one + mlp_out).astype(jnp.bfloat16)
    grad_proj_down = tall_product(hidden_low, cotangent)
    grad_bias_down = jnp.sum(cotangent.astype(jnp.float32), axis=0)
    (grad_pre,) = gelu_pull(wide_product(cotangent, proj_down))
    grad_pre_low = grad_pre.astype(jnp.bfloat16)
    grad_proj_up = tall_product(normed_two_low, grad_pre_low)
    grad_bias_up = jnp.sum(grad_pre_low.astype(jnp.float32), axis=0)
    grad_norm_terms = wide_product(grad_pre_low, proj_up)
    cot_f = cotangent.astype(jnp.float32)
    grad_normed_two = lax.psum(grad_norm_terms.astype(jnp.bfloat16), "mp").astype(jnp.float32)
    grad_hidden_part, grad_mlp_gain, grad_mlp_shift = norm_two_pull(grad_normed_two)
    grad_hidden_one = cot_f + grad_hidden_part
    grad_bias_out = jnp.sum(grad_hidden_one, axis=0)
    grad_attn_low = grad_hidden_one.astype(jnp.bfloat16)
    grad_proj_out = tall_product(gated_low, grad_attn_low)
    grad_gated = wide_product(grad_attn_low, proj_out)
    grad_queries, grad_conv, grad_mixed_direct, grad_skip_gain = gate_pull(grad_gated)
    regathered = lax.all_gather(long_taps, "dp", axis=0, tiled=True)
    kernel_back, kernel_pull_back = jax.vjp(
        build_kernel, regathered.astype(jnp.float32), decay_rates
    )
    grad_mixed_conv, grad_kernel = long_conv_back(
        grad_conv, mixed_in, kernel_back, mask_one, mask_two
    )
    grad_taps_full, grad_decay_rates = kernel_pull_back(grad_kernel)
    grad_streams, grad_short_taps = short_pull((grad_queries, grad_mixed_direct + grad_mixed_conv))
    grad_streams_low = grad_streams.reshape(seq_len, 3 * channels).astype(jnp.bfloat16)
    grad_proj_in = tall_product(normed_low, grad_streams_low).reshape(width, 3, channels)
    grad_bias_in = jnp.sum(grad_streams_low.astype(jnp.float32), axis=0).reshape(3, channels)
    grad_normed = lax.psum(
        wide_product(grad_streams_low, proj_flat).astype(jnp.bfloat16), "mp"
    ).astype(jnp.float32)
    grad_tokens_part, grad_mix_gain, grad_mix_shift = norm_pull(grad_normed)
    input_grad = grad_hidden_one + grad_tokens_part
    grad_long_taps = lax.psum_scatter(
        grad_taps_full.astype(jnp.bfloat16), "dp", scatter_dimension=0, tiled=True
    ).astype(jnp.float32)
    (
        grad_mix_gain,
        grad_mix_shift,
        grad_proj_in,
        grad_bias_in,
        grad_short_taps,
        grad_decay_rates,
        grad_skip_gain,
        grad_proj_out,
        grad_bias_out,
        grad_mlp_gain,
        grad_mlp_shift,
        grad_proj_up,
        grad_bias_up,
        grad_proj_down,
        grad_bias_down,
    ) = (
        lax.psum(grad_mix_gain.astype(jnp.bfloat16), "dp").astype(jnp.float32),
        lax.psum(grad_mix_shift.astype(jnp.bfloat16), "dp").astype(jnp.float32),
        lax.psum(grad_proj_in.astype(jnp.bfloat16), "dp").astype(jnp.float32),
        lax.psum(grad_bias_in.astype(jnp.bfloat16), "dp").astype(jnp.float32),
        lax.psum(grad_short_taps.astype(jnp.bfloat16), "dp").astype(jnp.float32),
        lax.psum(grad_decay_rates.astype(jnp.bfloat16), "dp").astype(jnp.float32),
        lax.psum(grad_skip_gain.astype(jnp.bfloat16), "dp").astype(jnp.float32),
        lax.psum(grad_proj_out.astype(jnp.bfloat16), "dp").astype(jnp.float32),
        lax.psum(grad_bias_out.astype(jnp.bfloat16), "dp").astype(jnp.float32),
        lax.psum(grad_mlp_gain.astype(jnp.bfloat16), "dp").astype(jnp.float32),
        lax.psum(grad_mlp_shift.astype(jnp.bfloat16), "dp").astype(jnp.float32),
        lax.psum(grad_proj_up.astype(jnp.bfloat16), "dp").astype(jnp.float32),
        lax.psum(grad_bias_up.astype(jnp.bfloat16), "dp").astype(jnp.float32),
        lax.psum(grad_proj_down.astype(jnp.bfloat16), "dp").astype(jnp.float32),
        lax.psum(grad_bias_down.astype(jnp.bfloat16), "dp").astype(jnp.float32),
    )
    return (
        output,
        input_grad,
        grad_mix_gain,
        grad_mix_shift,
        grad_proj_in,
        grad_bias_in,
        grad_short_taps,
        grad_long_taps,
        grad_decay_rates,
        grad_skip_gain,
        grad_proj_out,
        grad_bias_out,
        grad_mlp_gain,
        grad_mlp_shift,
        grad_proj_up,
        grad_bias_up,
        grad_proj_down,
        grad_bias_down,
    )


def solution(mesh):
    in_specs = (
        P("dp", None),
        P("dp", None),
        P(),
        P(),
        P(None, None, "mp"),
        P(None, "mp"),
        P(None, None, "mp"),
        P("dp", "mp"),
        P("mp"),
        P("mp"),
        P("mp", None),
        P(),
        P(),
        P(),
        P(None, "mp"),
        P("mp"),
        P("mp", None),
        P(),
        P("dp", None),
    )
    out_specs = (
        P("dp", None),
        P("dp", None),
        P(),
        P(),
        P(None, None, "mp"),
        P(None, "mp"),
        P(None, None, "mp"),
        P("dp", "mp"),
        P("mp"),
        P("mp"),
        P("mp", None),
        P(),
        P(),
        P(),
        P(None, "mp"),
        P("mp"),
        P("mp", None),
        P(),
    )
    return jax.shard_map(
        per_device, mesh=mesh, in_specs=in_specs, out_specs=out_specs, check_vma=False
    )
```

profile of v0, /device:TPU:0, one launch (start us, length us, event | category | flops | bytes accessed | tf_op | source)
XLA Modules:
  0.0 1298.6 jit_solution(12647565833582045572)
XLA Ops:
  19.3 33.9 %all_gather.4 = bf16[2048,192]{0,1:T(8,128)(2,1)S(1)} all-gather(bf16[256,192]{0,1:T(8,128)(2,1)S(1)} %copy-done.53), channel_id=1, replica_groups=mesh['dp'=8,'mp'=4] {'dp'}, dimensions={0}, use_global_device_ids=true | all-gather | bytes 884736 | tf_op jit(solution)/shard_map/all_gather | solution.py:217
  69.1 5.8 copy.51
  74.9 6.4 reshape.291
  81.2 6.4 dot_general.122
  87.6 16.4 %fusion.51 = f32[64,64,576]{2,0,1:T(8,128)} fusion(f32[64,576,32]{1,0,2:T(8,128)} %dot_general.122), kind=kOutput, calls=%fused_computation.95 | convolution fusion | flops 905998336 | bytes 14155776 | tf_op jit(solution)/shard_map/dot_general | solution.py:65
  104.1 20.2 %multiply_add_fusion.1 = (f32[64,64,576]{2,0,1:T(8,128)}, f32[64,64,576]{2,0,1:T(8,128)S(1)}) fusion(f32[64,64,576]{2,0,1:T(8,128)} %fusion.51, f32[64,64]{0,1:T(8,128)S(1)} %copy.55, f32[64,64]{0,1:T(8,128)S(1)} %copy.53, f32[64,576,32]{1,0,2:T(8,128)} %dot_general.122), kind=kOutput, calls=%fused_computation.23 | convolution fusion | flops 922513408 | bytes 33062912 | tf_op jit(solution)/shard_map/dot_general | solution.py:65
  124.3 21.2 %fusion.10 = f32[64,576,64]{1,2,0:T(8,128)} fusion(f32[64,64,576]{2,0,1:T(8,128)S(1)} %get-tuple-element.76), kind=kOutput, calls=%fused_computation.24 | convolution fusion | flops 1811996672 | bytes 18874368 | tf_op jit(solution)/shard_map/jn,knc->kjc/dot_general | solution.py:71
  145.5 21.2 %fusion.12 = f32[64,576,64]{1,2,0:T(8,128)} fusion(f32[64,64,576]{2,0,1:T(8,128)S(1)} %get-tuple-element.76), kind=kOutput, calls=%fused_computation.26 | convolution fusion | flops 1811996672 | bytes 18874368 | tf_op jit(solution)/shard_map/jn,knc->kjc/dot_general | solution.py:71
  166.7 23.6 %subtract_bitcast_fusion.2 = f32[64,64,576]{2,1,0:T(8,128)} fusion(f32[64,576,64]{1,2,0:T(8,128)} %fusion.10, f32[64,64,576]{2,0,1:T(8,128)} %get-tuple-element.75), kind=kOutput, calls=%fused_computation.20 | convolution fusion | flops 1814355968 | bytes 28311552 | tf_op jit(solution)/shard_map/jn,knc->kjc/dot_general | solution.py:71
  190.3 22.4 %add_bitcast_fusion.2 = f32[64,64,576]{2,1,0:T(8,128)S(1)} fusion(f32[64,576,64]{1,2,0:T(8,128)} %fusion.12, f32[64,64,576]{2,0,1:T(8,128)} %get-tuple-element.75), kind=kOutput, calls=%fused_computation.21 | convolution fusion | flops 1814355968 | bytes 28311552 | tf_op jit(solution)/shard_map/jn,knc->kjc/dot_general | solution.py:71
  217.0 4.5 tile.16
  221.5 10.7 tile.17
  234.4 4.4 tile.18
  238.8 11.1 tile.19
  249.9 9.6 multiply_subtract_fusion.5
  259.6 7.9 fusion.93
  267.4 7.8 fusion.105
  275.2 7.9 fusion.95
  283.1 14.9 %multiply_add_fusion.4 = (f32[64,384,64]{1,2,0:T(8,128)}, f32[64,384,64]{1,2,0:T(8,128)}) fusion(f32[64,64]{1,0:T(8,128)S(1)} %get-tuple-element.98, f32[64,64]{1,0:T(8,128)S(1)} %get-tuple-element.99, f32[64,384,64]{1,2,0:T(8,128)} %fusion.93, f32[64,384,64]{1,2,0:T(8,128)} %fusion.105, f32[64,384,64]{1,2,0:T(8,128)} %fusion.95, ...), kind=kOutput, calls=%fused_computation.90 | convolution fusion | flops 1220599808 | bytes 37781504 | tf_op jit(solution)/shard_map/jn,knc->kjc/dot_general | solution.py:71
  298.0 6.5 copy.80
  311.7 5.5 fusion.1
  320.4 4.9 fusion.291
  338.8 69.5 %all-reduce.22.cloned.1.call-done = bf16[2048,768]{1,0:T(8,128)(2,1)} async-done(((bf16[2048,768]{1,0:T(8,128)(2,1)}), bf16[2048,768]{1,0:T(8,128)(2,1)}) %all-reduce.22.cloned.1.call-update) | async-done | bytes 3145744 | tf_op jit(solution)/shard_map/psum | solution.py:223
  419.0 19.1 %fusion.283 = (bf16[768]{0:T(1024)(128)(2,1)}, bf16[2048,768]{1,0:T(8,128)(2,1)S(1)}, f32[2048,768]{1,0:T(8,128)}) fusion(f32[2048,768]{1,0:T(8,128)S(1)} %fusion.278, f32[768]{0:T(1024)S(1)} %copy-done.82, bf16[2048,768]{1,0:T(8,128)(2,1)S(1)} %copy-done.24, bf16[768,768]{1,0:T(8,128)(2,1)S(1)} %copy-done), kind=kOutput, calls=%fused_computation.369 | convolution fusion | flops 2532310272 | bytes 20058624 | tf_op jit(solution)/shard_map/dot_general | solution.py:59
  443.8 5.5 multiply_convert_fusion
  455.4 57.0 %all-reduce.24.cloned.1.call-done = bf16[2048,768]{1,0:T(8,128)(2,1)} async-done(((bf16[2048,768]{1,0:T(8,128)(2,1)}), bf16[2048,768]{1,0:T(8,128)(2,1)}) %all-reduce.24.cloned.1.call-update) | async-done | bytes 3145744 | tf_op jit(solution)/shard_map/psum | solution.py:241
  512.4 5.6 fusion.40
  518.9 5.2 fusion.41
  528.5 5.6 multiply_reduce_fusion.4
  538.9 9.2 copy.62
  548.1 9.1 reshape.294
  557.1 8.9 dot_general.142
  566.0 25.4 %fusion.30 = f32[64,64,960]{2,0,1:T(8,128)} fusion(f32[64,960,32]{1,0,2:T(8,128)} %dot_general.142), kind=kOutput, calls=%fused_computation.46 | convolution fusion | flops 1509978112 | bytes 23592960 | tf_op jit(solution)/shard_map/dot_general | solution.py:65
  591.4 26.6 %multiply_add_fusion = (f32[64,64,960]{2,0,1:T(8,128)}, f32[64,64,960]{2,0,1:T(8,128)}) fusion(f32[64,64,960]{2,0,1:T(8,128)} %fusion.30, f32[64,64]{0,1:T(8,128)S(1)} %copy-done.40, f32[64,64]{0,1:T(8,128)S(1)} %copy-done.42, f32[64,960,32]{1,0,2:T(8,128)S(1)} %copy-done.10), kind=kOutput, calls=%fused_computation.7 | convolution fusion | flops 1537503232 | bytes 55083008 | tf_op jit(solution)/shard_map/dot_general | solution.py:65
  618.0 36.1 %fusion.2 = f32[64,960,64]{1,2,0:T(8,128)} fusion(f32[64,64,960]{2,0,1:T(8,128)} %get-tuple-element.68), kind=kOutput, calls=%fused_computation.8 | convolution fusion | flops 3019956224 | bytes 31457280 | tf_op jit(solution)/shard_map/jn,knc->kjc/dot_general | solution.py:71
  654.1 36.5 %fusion.4 = f32[64,960,64]{1,2,0:T(8,128)} fusion(f32[64,64,960]{2,0,1:T(8,128)} %get-tuple-element.68), kind=kOutput, calls=%fused_computation.10 | convolution fusion | flops 3019956224 | bytes 31457280 | tf_op jit(solution)/shard_map/jn,knc->kjc/dot_general | solution.py:71
  690.6 32.7 %subtract_bitcast_fusion = f32[64,64,960]{2,1,0:T(8,128)} fusion(f32[64,960,64]{1,2,0:T(8,128)} %fusion.2, f32[64,64,960]{2,0,1:T(8,128)} %get-tuple-element.67), kind=kOutput, calls=%fused_computation.4 | convolution fusion | flops 3023888384 | bytes 47185920 | tf_op jit(solution)/shard_map/jn,knc->kjc/dot_general | solution.py:71
  723.3 32.6 %add_bitcast_fusion = f32[64,64,960]{2,1,0:T(8,128)} fusion(f32[64,960,64]{1,2,0:T(8,128)} %fusion.4, f32[64,64,960]{2,0,1:T(8,128)} %get-tuple-element.67), kind=kOutput, calls=%fused_computation.5 | convolution fusion | flops 3023888384 | bytes 47185920 | tf_op jit(solution)/shard_map/jn,knc->kjc/dot_general | solution.py:71
  758.1 4.5 tile.40
  762.6 10.7 tile.41
  775.5 4.4 tile.42
  780.0 10.7 tile.43
  790.7 23.6 %multiply_add_fusion.3 = (f32[64,64,384]{2,1,0:T(8,128)}, f32[64,64,384]{2,1,0:T(8,128)}, f32[64,64,384]{2,1,0:T(8,128)}, f32[64,64,384]{2,1,0:T(8,128)}) fusion(f32[64,64,384]{2,1,0:T(8,128)} %tile.43, f32[64,64,384]{2,1,0:T(8,128)} %tile.41, f32[64,64,960]{2,1,0:T(8,128)} %subtract_bitcast_fusion, f32[64,64,960]{2,1,0:T(8,128)} %add_bitcast_fusion), kind=kLoop, calls=%fused_computation.71 | loop fusion | flops 18874368 | bytes 62914560 | tf_op jit(solution)/shard_map/add | solution.py:168
  814.3 4.7 slice_add_fusion
  819.5 12.4 fusion.26
  831.9 12.7 fusion.27
  844.6 4.6 slice_add_fusion.1
  851.2 12.4 fusion.28
  863.6 28.0 %add_bitcast_fusion.1 = (f32[64,64,576]{2,1,0:T(8,128)}, f32[64,64,576]{2,1,0:T(8,128)}) fusion(f32[64,64]{1,0:T(8,128)S(1)} %copy-done.36, f32[64,64]{1,0:T(8,128)S(1)} %copy-done.38, f32[64,576,64]{1,2,0:T(8,128)} %fusion.26, f32[64,576,64]{1,2,0:T(8,128)} %fusion.28, f32[64,576,64]{1,2,0:T(8,128)} %fusion.27, f32[64,64,192]{2,1,0:T(8,128)} %copy-done.16, ...), kind=kOutput, calls=%fused_computation.18 | convolution fusion | flops 1833230336 | bytes 56655872 | tf_op jit(solution)/shard_map/jn,knc->kjc/dot_general | solution.py:71
  891.6 11.9 reshape.296
  903.5 11.9 reshape.295
  915.5 7.7 fusion.160
  923.1 6.8 fusion
  929.9 6.6 div.72
  936.5 6.6 fusion.290
  961.0 5.3 multiply_reduce_fusion.3
  975.0 6.7 convolution_convert_fusion.3
  981.8 7.5 convolution_convert_fusion.4
  999.6 14.3 %reduce-scatter.2.cloned.1.call-done = bf16[256,192]{0,1:T(8,128)(2,1)} async-done(((bf16[2048,192]{0,1:T(8,128)(2,1)}), bf16[256,192]{0,1:T(8,128)(2,1)}) %reduce-scatter.2.cloned.1.call-update) | async-done | bytes 98320 | tf_op jit(solution)/shard_map/reduce_scatter | solution.py:266
  1015.5 120.2 %all-reduce.28.cloned.1.call-done = (bf16[2048,768]{1,0:T(8,128)(2,1)}, bf16[2048,768]{1,0:T(8,128)(2,1)}) async-done(((bf16[2048,768]{1,0:T(8,128)(2,1)}, bf16[2048,768]{1,0:T(8,128)(2,1)}), (bf16[2048,768]{1,0:T(8,128)(2,1)}, bf16[2048,768]{1,0:T(8,128)(2,1)})) %all-reduce.28.cloned.1.call-update) | async-done | bytes 6291472 | tf_op jit(solution)/shard_map/psum | solution.py:231
  1142.3 5.1 fusion.42
  1147.4 39.5 %all-reduce.14 = (bf16[768]{0:T(1024)(128)(2,1)S(1)}, bf16[768]{0:T(1024)(128)(2,1)S(1)}, bf16[3,192]{1,0:T(4,128)(2,1)S(1)}, bf16[3,3,192]{2,1,0:T(4,128)(2,1)S...) all-reduce(bf16[768]{0:T(1024)(128)(2,1)S(1)} %get-tuple-element.20, ...), channel_id=1, replica_groups=mesh['dp'=8,'mp'=4] {'dp'}, use_global_device_ids=true, to_apply=%region_13.14 | all-reduce | flops 8064 | bytes 32256 | tf_op jit(solution)/shard_map/psum | solution.py:286
  1193.4 12.7 add_add_fusion.2
  1206.1 76.8 %all-reduce.26.cloned.1.call-done = (bf16[768,3,192]{0,2,1:T(8,128)(2,1)}, bf16[192,768]{1,0:T(8,128)(2,1)}, bf16[768,768]{1,0:T(8,128)(2,1)}, bf16[768,768]{1,0:T(8,128)(2,1)}) async-done(((bf16[768,3,192]{0,2,1:T(8,128)(2,1)}, bf16[192,768]{1,0:T(8,128)(2,1)}, bf16[768,768]{1,0:T(8,128)(2,1)}, bf16[768,768]{1,0:T(8,128)(2,1)}), (bf16[768,3,192]{0,2,1:T(8,128)(2,1)}, bf16[192,768]{1,0:T(8,128)(2,1)}, ...) | async-done | bytes 3538960 | tf_op jit(solution)/shard_map/psum | solution.py:288
  (305 shorter events, 155.9 us)
Async XLA Ops:
  7.2 411.7 %copy-start = (bf16[768,768]{1,0:T(8,128)(2,1)S(1)}, bf16[768,768]{1,0:T(8,128)(2,1)}, u32[]{:S(2)}) copy-start(bf16[768,768]{1,0:T(8,128)(2,1)} %param.35) | copy-start | bytes 3538948
  7.2 11.9 copy-start.77
  7.2 12.1 copy-start.53
  7.2 401.1 %all-reduce.22.cloned.1.call-start = ((), (), s32[]{:S(2)}) async-start(), calls=%async_computation.1 | async-start | bytes 6291456 | tf_op jit(solution)/shard_map/psum | solution.py:223
  7.3 49.2 %copy-start.57 = (f32[2048]{0:T(1024)}, f32[2048]{0:T(1024)S(1)}, u32[]{:S(2)}) copy-start(f32[2048]{0:T(1024)S(1)} %iota_convert_fusion) | copy-start | bytes 24580
  9.3 49.7 %copy-start.63 = (f32[2048]{0:T(1024)}, f32[2048]{0:T(1024)S(1)}, u32[]{:S(2)}) copy-start(f32[2048]{0:T(1024)S(1)} %fusion.172) | copy-start | bytes 24580
  10.0 49.0 %copy-start.65 = (f32[2048]{0:T(1024)}, f32[2048]{0:T(1024)S(1)}, u32[]{:S(2)}) copy-start(f32[2048]{0:T(1024)S(1)} %get-tuple-element.97) | copy-start | bytes 24580
  10.0 524.2 %copy-start.45 = (f32[2048]{0:T(1024)}, f32[2048]{0:T(1024)S(1)}, u32[]{:S(2)}) copy-start(f32[2048]{0:T(1024)S(1)} %get-tuple-element.96) | copy-start | bytes 24580
  10.1 273.0 %copy-start.35 = (f32[64,64]{1,0:T(8,128)}, f32[64,64]{1,0:T(8,128)S(1)}, u32[]{:S(2)}) copy-start(f32[64,64]{1,0:T(8,128)S(1)} %get-tuple-element.98) | copy-start | bytes 49156
  10.1 273.0 %copy-start.37 = (f32[64,64]{1,0:T(8,128)}, f32[64,64]{1,0:T(8,128)S(1)}, u32[]{:S(2)}) copy-start(f32[64,64]{1,0:T(8,128)S(1)} %get-tuple-element.99) | copy-start | bytes 49156
  10.9 45.6 %copy-start.78 = (f32[192]{0:T(256)}, f32[192]{0:T(256)S(1)}, u32[]{:S(2)}) copy-start(f32[192]{0:T(256)S(1)} %neg.29) | copy-start | bytes 2308
  13.6 521.9 %copy-start.47 = (f32[2048]{0:T(1024)}, f32[2048]{0:T(1024)S(1)}, u32[]{:S(2)}) copy-start(f32[2048]{0:T(1024)S(1)} %fusion.174) | copy-start | bytes 24580
  16.0 40.5 %copy-start.69 = (f32[768]{0:T(1024)S(1)}, f32[768]{0:T(1024)}, u32[]{:S(2)}) copy-start(f32[768]{0:T(1024)} %param.21) | copy-start | bytes 9220
  16.0 40.5 %copy-start.89 = (bf16[768,3,192]{0,2,1:T(8,128)(2,1)S(1)}, bf16[768,3,192]{0,2,1:T(8,128)(2,1)}, u32[]{:S(2)}) copy-start(bf16[768,3,192]{0,2,1:T(8,128)(2,1)} %param.23) | copy-start | bytes 2654212
  16.0 40.5 %copy-start.93 = (f32[768]{0:T(1024)S(1)}, f32[768]{0:T(1024)}, u32[]{:S(2)}) copy-start(f32[768]{0:T(1024)} %param.22) | copy-start | bytes 9220
  16.0 42.9 %copy-start.43 = (f32[2048]{0:T(1024)}, f32[2048]{0:T(1024)S(1)}, u32[]{:S(2)}) copy-start(f32[2048]{0:T(1024)S(1)} %broadcast_multiply_fusion.5) | copy-start | bytes 24580
  19.0 39.9 %copy-start.61 = (f32[2048]{0:T(1024)}, f32[2048]{0:T(1024)S(1)}, u32[]{:S(2)}) copy-start(f32[2048]{0:T(1024)S(1)} %fusion.43) | copy-start | bytes 24580
  19.1 39.8 %copy-start.54 = (f32[2048]{0:T(1024)}, f32[2048]{0:T(1024)S(1)}, u32[]{:S(2)}) copy-start(f32[2048]{0:T(1024)S(1)} %fusion.175) | copy-start | bytes 24580
  19.1 39.9 %copy-start.71 = (f32[3,192]{1,0:T(4,128)}, f32[3,192]{1,0:T(4,128)S(1)}, u32[]{:S(2)}) copy-start(f32[3,192]{1,0:T(4,128)S(1)} %get-tuple-element.91) | copy-start | bytes 6916
  19.1 39.9 %copy-start.73 = (f32[3,192]{1,0:T(4,128)}, f32[3,192]{1,0:T(4,128)S(1)}, u32[]{:S(2)}) copy-start(f32[3,192]{1,0:T(4,128)S(1)} %get-tuple-element.93) | copy-start | bytes 6916
  19.1 39.9 %copy-start.75 = (f32[3,192]{1,0:T(4,128)}, f32[3,192]{1,0:T(4,128)S(1)}, u32[]{:S(2)}) copy-start(f32[3,192]{1,0:T(4,128)S(1)} %get-tuple-element.92) | copy-start | bytes 6916
  19.2 84.9 %copy-start.39 = (f32[64,64]{0,1:T(8,128)}, f32[64,64]{0,1:T(8,128)S(1)}, u32[]{:S(2)}) copy-start(f32[64,64]{0,1:T(8,128)S(1)} %copy.55) | copy-start | bytes 49156
  19.3 84.8 %copy-start.41 = (f32[64,64]{0,1:T(8,128)}, f32[64,64]{0,1:T(8,128)S(1)}, u32[]{:S(2)}) copy-start(f32[64,64]{0,1:T(8,128)S(1)} %copy.53) | copy-start | bytes 49156
  19.3 37.2 %copy-start.2 = (bf16[2048,768]{1,0:T(8,128)(2,1)S(1)}, bf16[2048,768]{1,0:T(8,128)(2,1)}, u32[]{:S(2)}) copy-start(bf16[2048,768]{1,0:T(8,128)(2,1)} %param.19) | copy-start | bytes 9437188
  320.4 10.4 copy-start.84
  328.1 7.9 copy-start.34
  335.1 73.2 %copy-start.51 = (f32[768]{0:T(1024)S(1)}, f32[768]{0:T(1024)}, u32[]{:S(2)}) copy-start(f32[768]{0:T(1024)} %param.30) | copy-start | bytes 9220
  338.7 76.3 %copy-start.67 = (f32[768]{0:T(1024)S(1)}, f32[768]{0:T(1024)}, u32[]{:S(2)}) copy-start(f32[768]{0:T(1024)} %param.31) | copy-start | bytes 9220
  338.7 76.3 %copy-start.91 = (f32[768]{0:T(1024)S(1)}, f32[768]{0:T(1024)}, u32[]{:S(2)}) copy-start(f32[768]{0:T(1024)} %param.32) | copy-start | bytes 9220
  338.7 173.7 %all-reduce.24.cloned.1.call-start = ((), (), s32[]{:S(2)}) async-start(), calls=%async_computation.2 | async-start | bytes 6291456 | tf_op jit(solution)/shard_map/psum | solution.py:241
  413.0 111.2 %copy-start.49 = (f32[2048]{0:T(1024)}, f32[2048]{0:T(1024)S(1)}, u32[]{:S(2)}) copy-start(f32[2048]{0:T(1024)S(1)} %broadcast_multiply_fusion.4) | copy-start | bytes 24580
  415.0 109.1 %copy-start.59 = (f32[2048]{0:T(1024)}, f32[2048]{0:T(1024)S(1)}, u32[]{:S(2)}) copy-start(f32[2048]{0:T(1024)S(1)} %fusion.176) | copy-start | bytes 24580
  419.0 19.1 %copy-start.30 = (f32[2048,768]{1,0:T(8,128)}, f32[2048,768]{1,0:T(8,128)S(1)}, u32[]{:S(2)}) copy-start(f32[2048,768]{1,0:T(8,128)S(1)} %fusion.278) | copy-start | bytes 18874372
  443.7 570.2 %reduce-scatter.2.cloned.1.call-start = ((), (), s32[]{:S(2)}) async-start(), calls=%async_computation.3 | async-start | bytes 884736 | tf_op jit(solution)/shard_map/reduce_scatter | solution.py:266
  566.0 25.4 %copy-start.10 = (f32[64,960,32]{1,0,2:T(8,128)S(1)}, f32[64,960,32]{1,0,2:T(8,128)}, u32[]{:S(2)}) copy-start(f32[64,960,32]{1,0,2:T(8,128)} %dot_general.142) | copy-start | bytes 23592964
  566.0 25.4 %copy-start.40 = (f32[64,64]{0,1:T(8,128)S(1)}, f32[64,64]{0,1:T(8,128)}, u32[]{:S(2)}) copy-start(f32[64,64]{0,1:T(8,128)} %copy-done.39) | copy-start | bytes 49156
  566.0 25.4 %copy-start.42 = (f32[64,64]{0,1:T(8,128)S(1)}, f32[64,64]{0,1:T(8,128)}, u32[]{:S(2)}) copy-start(f32[64,64]{0,1:T(8,128)} %copy-done.41) | copy-start | bytes 49156
  819.5 31.6 %slice-start.6 = ((s8[6291456]{0:T(1024)(128)(4,1)}), s8[4194304]{0:T(1024)(128)(4,1)S(1)}, s32[]{:S(2)}) async-start(s8[6291456]{0:T(1024)(128)(4,1)} %bitcast.171), calls=%async_computation.12 | async-start | bytes 8388608
  831.9 19.2 %slice-start.7 = ((s8[6291456]{0:T(1024)(128)(4,1)}), s8[2097152]{0:T(1024)(128)(4,1)S(1)}, s32[]{:S(2)}) async-start(s8[6291456]{0:T(1024)(128)(4,1)} %bitcast.171), calls=%async_computation.13 | async-start | bytes 4194304
  851.1 12.5 copy-start.36
  851.2 12.5 copy-start.38
  915.5 7.7 copy-start.17
  936.5 9.5 copy-start.22
  948.5 7.6 copy-start.20
  948.5 7.6 copy-start.46
  948.5 7.6 copy-start.48
  948.5 7.6 copy-start.85
  950.4 185.2 %all-reduce.28.cloned.1.call-start = ((), (), s32[]{:S(2)}) async-start(), calls=%async_computation.5 | async-start | bytes 12582912 | tf_op jit(solution)/shard_map/psum | solution.py:231
  953.3 7.7 slice-start
  974.7 7.0 copy-start.68
  974.7 7.0 copy-start.92
  974.8 308.2 %all-reduce.26.cloned.1.call-start = ((), (), s32[]{:S(2)}) async-start(), calls=%async_computation.4 | async-start | bytes 7077888 | tf_op jit(solution)/shard_map/psum | solution.py:288
  975.0 14.3 %slice-start.2 = ((s8[6291456]{0:T(1024)(128)(4,1)}), s8[4194304]{0:T(1024)(128)(4,1)S(1)}, s32[]{:S(2)}) async-start(s8[6291456]{0:T(1024)(128)(4,1)} %bitcast.169), calls=%async_computation.8 | async-start | bytes 8388608
  981.8 7.6 slice-start.3
  981.8 7.6 copy-start.27
  997.2 145.1 %copy-start.62 = (f32[2048]{0:T(1024)S(1)}, f32[2048]{0:T(1024)}, u32[]{:S(2)}) copy-start(f32[2048]{0:T(1024)} %copy-done.61) | copy-start | bytes 24580
  1138.1 9.3 copy-start.80
  1138.1 9.3 copy-start.81
  1138.1 9.3 copy-start.86
  1138.1 9.3 copy-start.87
  1138.1 55.3 %copy-start.56 = (f32[2048]{0:T(1024)S(1)}, f32[2048]{0:T(1024)}, u32[]{:S(2)}) copy-start(f32[2048]{0:T(1024)} %copy-done.54) | copy-start | bytes 24580
  1138.1 55.3 %copy-start.83 = (f32[768]{0:T(1024)S(1)}, f32[768]{0:T(1024)}, u32[]{:S(2)}) copy-start(f32[768]{0:T(1024)} %param.36) | copy-start | bytes 9220
  1193.4 98.4 %copy-start.1 = (bf16[768,768]{1,0:T(8,128)(2,1)S(1)}, bf16[768,768]{1,0:T(8,128)(2,1)}, u32[]{:S(2)}) copy-start(bf16[768,768]{1,0:T(8,128)(2,1)} %param.35) | copy-start | bytes 3538948
  1282.9 7.3 copy-start.33
  (47 other events, 186.1 us)
Sparse Core Ops, SparseCore 0:
  338.8 69.4 all-reduce.21
  443.8 68.5 all-reduce.23
  950.6 63.2 reduce-scatter.1
  1016.8 118.7 all-reduce.27
  1141.7 141.1 all-reduce.25
where the time goes:
time: 1310 us; the launch traced here: 1300 us
  matrix products  508 us (39%)
  waiting for transfers between devices  338 us (26%)
  local copies, waits for them, and re-layouts  199 us (15%)
  other arithmetic  163 us (12%)
  blocking collectives  73.4 us (6%)
  between operations  16.7 us (1%)
    dot_general x16, matrix products, across(): jnp.einsum('jn,knc->kjc', table, values, precision=lax.Precision.HIGHEST,...  330 us
    psum x1, waiting for transfers between devices, per_device(): lax.psum(down_terms.astype(jnp.bfloat16), 'mp').astype(jnp.float32)  120 us
    dot_general x8, matrix products, exact_product(): jnp.dot(lhs_mat, rhs_mat, precision=lax.Precision.HIGHEST, preferred_elem...  112 us
    psum x1, waiting for transfers between devices, per_device(): lax.psum(grad_proj_in.astype(jnp.bfloat16), 'dp').astype(jnp.float32)  76.8 us
    psum x1, waiting for transfers between devices, per_device(): lax.psum(attn_terms.astype(jnp.bfloat16), 'mp').astype(jnp.float32)  69.5 us
    psum x1, waiting for transfers between devices, per_device(): lax.psum(grad_norm_terms.astype(jnp.bfloat16), 'mp').astype(jnp.float32)  57 us
    psum x1, blocking collectives, per_device(): lax.psum(grad_mix_gain.astype(jnp.bfloat16), 'dp').astype(jnp.float32)  39.5 us
    unnamed x213, local copies, waits for them, and re-layouts  38.2 us
  transfers between devices with their start and end apart: 5, of which 5 were waited for; matrix products, arithmetic and copies ran while one was open for 7% of the time, Pallas kernels for 0%

commit v1 on v0

--- a/solution.py
+++ b/solution.py
@@ -4,6 +4,12 @@
 import jax.numpy as jnp
 from jax import lax
 from jax.sharding import PartitionSpec as P
+
+
+def gather_and_add(x, axis):
+    blocks = lax.all_gather(x, axis, axis=0, tiled=False)
+    summed = blocks.sum(axis=0)
+    return summed
 
 
 def layer_norm(values, scale_vec, shift_vec):
@@ -228,7 +234,7 @@
     hidden, gelu_pull = jax.vjp(gelu_exact, pre_act)
     hidden_low = hidden.astype(jnp.bfloat16)
     down_terms = plain_product(hidden_low, proj_down)
-    mlp_out = lax.psum(down_terms.astype(jnp.bfloat16), "mp").astype(jnp.float32) + bias_down
+    mlp_out = gather_and_add(down_terms.astype(jnp.bfloat16), "mp").astype(jnp.float32) + bias_down
     output = (hidden_one + mlp_out).astype(jnp.bfloat16)
     grad_proj_down = tall_product(hidden_low, cotangent)
     grad_bias_down = jnp.sum(cotangent.astype(jnp.float32), axis=0)

time: 1310 us -> 1360 us (1.038)
  waiting for transfers between devices: 338 us -> 381 us
    psum x1, waiting for transfers between devices: 120 us -> 32.9 us  [per_device(): lax.psum(wide_product(grad_streams_low, proj_flat).astype(jnp.bfloat16),...]
    all_gather x0 -> x1, waiting for transfers between devices: none -> 72.5 us  [gather_and_add(): blocks = lax.all_gather(x, axis, axis=0, tiled=False)]
    psum x1, waiting for transfers between devices: 76.8 us -> 136 us  [per_device(): lax.psum(grad_proj_in.astype(jnp.bfloat16), 'dp').astype(jnp.float32)]
    unnamed x213 -> x207, local copies, waits for them, and re-layouts: 38.2 us -> 42.9 us
  transfers between devices with their start and end apart: 5 -> 6, of which waited for: 5 -> 6; matrix products, arithmetic and copies ran while one was open for 7% -> 6% of each run, Pallas kernels for 0% -> 0%
where the time goes in v1:
time: 1360 us; the launch traced here: 1350 us
  matrix products  512 us (38%)
  waiting for transfers between devices  381 us (28%)
  local copies, waits for them, and re-layouts  204 us (15%)
  other arithmetic  170 us (12%)
  blocking collectives  71 us (5%)
  between operations  16.9 us (1%)
    dot_general x16, matrix products, across(): jnp.einsum('jn,knc->kjc', table, values, precision=lax.Precision.HIGHEST,...  331 us
    psum x1, waiting for transfers between devices, per_device(): lax.psum(grad_proj_in.astype(jnp.bfloat16), 'dp').astype(jnp.float32)  136 us
    dot_general x8, matrix products, exact_product(): jnp.dot(lhs_mat, rhs_mat, precision=lax.Precision.HIGHEST, preferred_elem...  112 us
    all_gather x1, waiting for transfers between devices, gather_and_add(): blocks = lax.all_gather(x, axis, axis=0, tiled=False)  72.5 us
    psum x1, waiting for transfers between devices, per_device(): lax.psum(attn_terms.astype(jnp.bfloat16), 'mp').astype(jnp.float32)  69.5 us
    psum x1, waiting for transfers between devices, per_device(): lax.psum(grad_norm_terms.astype(jnp.bfloat16), 'mp').astype(jnp.float32)  57.5 us
    unnamed x207, local copies, waits for them, and re-layouts  42.9 us
    psum x1, blocking collectives, per_device(): lax.psum(grad_mix_gain.astype(jnp.bfloat16), 'dp').astype(jnp.float32)  37.2 us
  transfers between devices with their start and end apart: 6, of which 6 were waited for; matrix products, arithmetic and copies ran while one was open for 6% of the time, Pallas kernels for 0%

profile of v1, /device:TPU:0, one launch (start us, length us, event | category | flops | bytes accessed | tf_op | source)
XLA Modules:
  0.0 1354.3 jit_solution(7325912070939864586)
XLA Ops:
  19.3 33.9 %all_gather.10 = bf16[2048,192]{0,1:T(8,128)(2,1)S(1)} all-gather(bf16[256,192]{0,1:T(8,128)(2,1)S(1)} %copy-done.53), channel_id=1, replica_groups=mesh['dp'=8,'mp'=4] {'dp'}, dimensions={0}, use_global_device_ids=true | all-gather | bytes 884736 | tf_op jit(solution)/shard_map/all_gather | solution.py:223
  70.7 5.8 copy.51
  76.4 6.4 reshape.291
  82.8 6.4 dot_general.122
  89.2 16.4 %fusion.51 = f32[64,64,576]{2,0,1:T(8,128)} fusion(f32[64,576,32]{1,0,2:T(8,128)} %dot_general.122), kind=kOutput, calls=%fused_computation.95 | convolution fusion | flops 905998336 | bytes 14155776 | tf_op jit(solution)/shard_map/dot_general | solution.py:71
  105.6 20.2 %multiply_add_fusion.1 = (f32[64,64,576]{2,0,1:T(8,128)}, f32[64,64,576]{2,0,1:T(8,128)S(1)}) fusion(f32[64,64,576]{2,0,1:T(8,128)} %fusion.51, f32[64,64]{0,1:T(8,128)S(1)} %copy.55, f32[64,64]{0,1:T(8,128)S(1)} %copy.53, f32[64,576,32]{1,0,2:T(8,128)} %dot_general.122), kind=kOutput, calls=%fused_computation.23 | convolution fusion | flops 922513408 | bytes 33062912 | tf_op jit(solution)/shard_map/dot_general | solution.py:71
  125.8 21.3 %fusion.10 = f32[64,576,64]{1,2,0:T(8,128)} fusion(f32[64,64,576]{2,0,1:T(8,128)S(1)} %get-tuple-element.74), kind=kOutput, calls=%fused_computation.24 | convolution fusion | flops 1811996672 | bytes 18874368 | tf_op jit(solution)/shard_map/jn,knc->kjc/dot_general | solution.py:77
  147.1 21.4 %fusion.12 = f32[64,576,64]{1,2,0:T(8,128)} fusion(f32[64,64,576]{2,0,1:T(8,128)S(1)} %get-tuple-element.74), kind=kOutput, calls=%fused_computation.26 | convolution fusion | flops 1811996672 | bytes 18874368 | tf_op jit(solution)/shard_map/jn,knc->kjc/dot_general | solution.py:77
  168.5 23.3 %subtract_bitcast_fusion.2 = f32[64,64,576]{2,1,0:T(8,128)} fusion(f32[64,576,64]{1,2,0:T(8,128)} %fusion.10, f32[64,64,576]{2,0,1:T(8,128)} %get-tuple-element.73), kind=kOutput, calls=%fused_computation.20 | convolution fusion | flops 1814355968 | bytes 28311552 | tf_op jit(solution)/shard_map/jn,knc->kjc/dot_general | solution.py:77
  191.8 22.7 %add_bitcast_fusion.2 = f32[64,64,576]{2,1,0:T(8,128)S(1)} fusion(f32[64,576,64]{1,2,0:T(8,128)} %fusion.12, f32[64,64,576]{2,0,1:T(8,128)} %get-tuple-element.73), kind=kOutput, calls=%fused_computation.21 | convolution fusion | flops 1814355968 | bytes 28311552 | tf_op jit(solution)/shard_map/jn,knc->kjc/dot_general | solution.py:77
  218.6 4.5 tile.16
  223.2 10.7 tile.17
  240.6 10.9 tile.19
  251.4 9.5 multiply_subtract_fusion.5
  261.0 7.9 fusion.93
  268.9 7.8 fusion.105
  276.6 7.9 fusion.95
  284.5 14.9 %multiply_add_fusion.4 = (f32[64,384,64]{1,2,0:T(8,128)}, f32[64,384,64]{1,2,0:T(8,128)}) fusion(f32[64,64]{1,0:T(8,128)S(1)} %get-tuple-element.95, f32[64,64]{1,0:T(8,128)S(1)} %get-tuple-element.96, f32[64,384,64]{1,2,0:T(8,128)} %fusion.93, f32[64,384,64]{1,2,0:T(8,128)} %fusion.105, f32[64,384,64]{1,2,0:T(8,128)} %fusion.95, ...), kind=kOutput, calls=%fused_computation.90 | convolution fusion | flops 1220599808 | bytes 37781504 | tf_op jit(solution)/shard_map/jn,knc->kjc/dot_general | solution.py:77
  299.5 6.5 copy.80
  313.1 5.7 fusion.1
  322.1 4.9 fusion.291
  340.4 69.5 %all-reduce.21.cloned.1.call-done = bf16[2048,768]{1,0:T(8,128)(2,1)} async-done(((bf16[2048,768]{1,0:T(8,128)(2,1)}), bf16[2048,768]{1,0:T(8,128)(2,1)}) %all-reduce.21.cloned.1.call-update) | async-done | bytes 3145744 | tf_op jit(solution)/shard_map/psum | solution.py:229
  420.5 19.1 %fusion.283 = (bf16[768]{0:T(1024)(128)(2,1)}, bf16[2048,768]{1,0:T(8,128)(2,1)S(1)}, f32[2048,768]{1,0:T(8,128)}) fusion(f32[2048,768]{1,0:T(8,128)S(1)} %fusion.278, f32[768]{0:T(1024)S(1)} %copy-done.82, bf16[2048,768]{1,0:T(8,128)(2,1)S(1)} %copy-done.22, bf16[768,768]{1,0:T(8,128)(2,1)S(1)} %copy-done), kind=kOutput, calls=%fused_computation.369 | convolution fusion | flops 2532310272 | bytes 20058624 | tf_op jit(solution)/shard_map/dot_general | solution.py:65
  445.3 5.5 multiply_convert_fusion
  456.5 57.5 %all-reduce.23.cloned.1.call-done = bf16[2048,768]{1,0:T(8,128)(2,1)} async-done(((bf16[2048,768]{1,0:T(8,128)(2,1)}), bf16[2048,768]{1,0:T(8,128)(2,1)}) %all-reduce.23.cloned.1.call-update) | async-done | bytes 3145744 | tf_op jit(solution)/shard_map/psum | solution.py:247
  513.9 5.2 fusion.40
  519.1 6.7 fusion.41
  525.8 72.5 %all-gather.3.cloned.1.call-done = bf16[8192,768]{1,0:T(8,128)(2,1)} async-done(((bf16[2048,768]{1,0:T(8,128)(2,1)}), bf16[8192,768]{1,0:T(8,128)(2,1)}) %all-gather.3.cloned.1.call-update) | async-done | bytes 12582928 | tf_op jit(solution)/shard_map/all_gather | solution.py:10
  598.3 9.0 reduce_sum.231
  607.3 10.2 fusion.285
  617.5 5.6 multiply_reduce_fusion.4
  627.8 9.1 copy.62
  636.9 9.0 reshape.294
  645.9 8.9 dot_general.142
  654.8 25.8 %fusion.30 = f32[64,64,960]{2,0,1:T(8,128)} fusion(f32[64,960,32]{1,0,2:T(8,128)} %dot_general.142), kind=kOutput, calls=%fused_computation.46 | convolution fusion | flops 1509978112 | bytes 23592960 | tf_op jit(solution)/shard_map/dot_general | solution.py:71
  680.7 26.3 %multiply_add_fusion = (f32[64,64,960]{2,0,1:T(8,128)}, f32[64,64,960]{2,0,1:T(8,128)}) fusion(f32[64,64,960]{2,0,1:T(8,128)} %fusion.30, f32[64,64]{0,1:T(8,128)S(1)} %copy-done.40, f32[64,64]{0,1:T(8,128)S(1)} %copy-done.42, f32[64,960,32]{1,0,2:T(8,128)S(1)} %copy-done.8), kind=kOutput, calls=%fused_computation.7 | convolution fusion | flops 1537503232 | bytes 55083008 | tf_op jit(solution)/shard_map/dot_general | solution.py:71
  707.0 36.1 %fusion.2 = f32[64,960,64]{1,2,0:T(8,128)} fusion(f32[64,64,960]{2,0,1:T(8,128)} %get-tuple-element.66), kind=kOutput, calls=%fused_computation.8 | convolution fusion | flops 3019956224 | bytes 31457280 | tf_op jit(solution)/shard_map/jn,knc->kjc/dot_general | solution.py:77
  743.1 36.3 %fusion.4 = f32[64,960,64]{1,2,0:T(8,128)} fusion(f32[64,64,960]{2,0,1:T(8,128)} %get-tuple-element.66), kind=kOutput, calls=%fused_computation.10 | convolution fusion | flops 3019956224 | bytes 31457280 | tf_op jit(solution)/shard_map/jn,knc->kjc/dot_general | solution.py:77
  779.4 32.7 %subtract_bitcast_fusion = f32[64,64,960]{2,1,0:T(8,128)} fusion(f32[64,960,64]{1,2,0:T(8,128)} %fusion.2, f32[64,64,960]{2,0,1:T(8,128)} %get-tuple-element.65), kind=kOutput, calls=%fused_computation.4 | convolution fusion | flops 3023888384 | bytes 47185920 | tf_op jit(solution)/shard_map/jn,knc->kjc/dot_general | solution.py:77
  812.1 32.7 %add_bitcast_fusion = f32[64,64,960]{2,1,0:T(8,128)} fusion(f32[64,960,64]{1,2,0:T(8,128)} %fusion.4, f32[64,64,960]{2,0,1:T(8,128)} %get-tuple-element.65), kind=kOutput, calls=%fused_computation.5 | convolution fusion | flops 3023888384 | bytes 47185920 | tf_op jit(solution)/shard_map/jn,knc->kjc/dot_general | solution.py:77
  851.5 10.7 tile.41
  868.8 10.8 tile.43
  879.6 22.7 %multiply_add_fusion.3 = (f32[64,64,384]{2,1,0:T(8,128)}, f32[64,64,384]{2,1,0:T(8,128)}, f32[64,64,384]{2,1,0:T(8,128)}, f32[64,64,384]{2,1,0:T(8,128)}) fusion(f32[64,64,384]{2,1,0:T(8,128)} %tile.43, f32[64,64,384]{2,1,0:T(8,128)} %tile.41, f32[64,64,960]{2,1,0:T(8,128)} %subtract_bitcast_fusion, f32[64,64,960]{2,1,0:T(8,128)} %add_bitcast_fusion), kind=kLoop, calls=%fused_computation.71 | loop fusion | flops 18874368 | bytes 62914560 | tf_op jit(solution)/shard_map/add | solution.py:174
  902.3 4.7 slice_add_fusion
  907.5 12.5 fusion.26
  920.0 12.7 fusion.27
  932.7 4.6 slice_add_fusion.1
  939.3 12.6 fusion.28
  952.0 28.1 %add_bitcast_fusion.1 = (f32[64,64,576]{2,1,0:T(8,128)}, f32[64,64,576]{2,1,0:T(8,128)}) fusion(f32[64,64]{1,0:T(8,128)S(1)} %copy-done.36, f32[64,64]{1,0:T(8,128)S(1)} %copy-done.38, f32[64,576,64]{1,2,0:T(8,128)} %fusion.26, f32[64,576,64]{1,2,0:T(8,128)} %fusion.28, f32[64,576,64]{1,2,0:T(8,128)} %fusion.27, f32[64,64,192]{2,1,0:T(8,128)} %copy-done.14, ...), kind=kOutput, calls=%fused_computation.18 | convolution fusion | flops 1833230336 | bytes 56655872 | tf_op jit(solution)/shard_map/jn,knc->kjc/dot_general | solution.py:77
  980.1 11.9 reshape.296
  992.0 11.9 reshape.295
  1003.9 7.7 fusion.160
  1011.6 6.7 fusion
  1018.3 6.6 div.72
  1024.9 6.5 fusion.290
  1042.0 5.3 multiply_reduce_fusion.3
  1057.3 8.5 convolution_convert_fusion.4
  1073.4 6.8 convolution_convert_fusion.3
  1092.9 32.9 %all-reduce.25.cloned.1.call-done = bf16[2048,768]{1,0:T(8,128)(2,1)} async-done(((bf16[2048,768]{1,0:T(8,128)(2,1)}), bf16[2048,768]{1,0:T(8,128)(2,1)}) %all-reduce.25.cloned.1.call-update) | async-done | bytes 3145744 | tf_op jit(solution)/shard_map/psum | solution.py:267
  1132.1 5.1 fusion.42
  1137.2 37.2 %all-reduce.14 = (bf16[768]{0:T(1024)(128)(2,1)S(1)}, bf16[768]{0:T(1024)(128)(2,1)S(1)}, bf16[3,192]{1,0:T(4,128)(2,1)S(1)}, bf16[3,3,192]{2,1,0:T(4,128)(2,1)S...) all-reduce(bf16[768]{0:T(1024)(128)(2,1)S(1)} %get-tuple-element.20, ...), channel_id=1, replica_groups=mesh['dp'=8,'mp'=4] {'dp'}, use_global_device_ids=true, to_apply=%region_13.14 | all-reduce | flops 8064 | bytes 32256 | tf_op jit(solution)/shard_map/psum | solution.py:292
  1180.9 12.0 reduce-scatter.2.cloned.1.call-done
  1194.4 7.5 add_add_fusion.2
  1202.0 136.4 %all-reduce.27.cloned.1.call-done = (bf16[768,3,192]{0,2,1:T(8,128)(2,1)}, bf16[192,768]{1,0:T(8,128)(2,1)}, bf16[768,768]{1,0:T(8,128)(2,1)}, bf16[768,768]{1,0:T(8,128)(2,1)}) async-done(((bf16[768,3,192]{0,2,1:T(8,128)(2,1)}, bf16[192,768]{1,0:T(8,128)(2,1)}, bf16[768,768]{1,0:T(8,128)(2,1)}, bf16[768,768]{1,0:T(8,128)(2,1)}), (bf16[768,3,192]{0,2,1:T(8,128)(2,1)}, bf16[192,768]{1,0:T(8,128)(2,1)}, ...) | async-done | bytes 3538960 | tf_op jit(solution)/shard_map/psum | solution.py:294
  (302 shorter events, 168.6 us)
Async XLA Ops:
  7.2 413.3 %copy-start = (bf16[768,768]{1,0:T(8,128)(2,1)S(1)}, bf16[768,768]{1,0:T(8,128)(2,1)}, u32[]{:S(2)}) copy-start(bf16[768,768]{1,0:T(8,128)(2,1)} %param.35) | copy-start | bytes 3538948
  7.2 11.9 copy-start.77
  7.2 12.1 copy-start.53
  7.2 402.7 %all-reduce.21.cloned.1.call-start = ((), (), s32[]{:S(2)}) async-start(), calls=%async_computation.1 | async-start | bytes 6291456 | tf_op jit(solution)/shard_map/psum | solution.py:229
  7.3 49.2 %copy-start.58 = (f32[2048]{0:T(1024)}, f32[2048]{0:T(1024)S(1)}, u32[]{:S(2)}) copy-start(f32[2048]{0:T(1024)S(1)} %iota_convert_fusion) | copy-start | bytes 24580
  9.3 49.6 %copy-start.62 = (f32[2048]{0:T(1024)}, f32[2048]{0:T(1024)S(1)}, u32[]{:S(2)}) copy-start(f32[2048]{0:T(1024)S(1)} %fusion.172) | copy-start | bytes 24580
  10.0 49.0 %copy-start.64 = (f32[2048]{0:T(1024)}, f32[2048]{0:T(1024)S(1)}, u32[]{:S(2)}) copy-start(f32[2048]{0:T(1024)S(1)} %get-tuple-element.94) | copy-start | bytes 24580
  10.0 613.1 %copy-start.47 = (f32[2048]{0:T(1024)}, f32[2048]{0:T(1024)S(1)}, u32[]{:S(2)}) copy-start(f32[2048]{0:T(1024)S(1)} %get-tuple-element.93) | copy-start | bytes 24580
  10.1 274.4 %copy-start.35 = (f32[64,64]{1,0:T(8,128)}, f32[64,64]{1,0:T(8,128)S(1)}, u32[]{:S(2)}) copy-start(f32[64,64]{1,0:T(8,128)S(1)} %get-tuple-element.95) | copy-start | bytes 49156
  10.1 274.4 %copy-start.37 = (f32[64,64]{1,0:T(8,128)}, f32[64,64]{1,0:T(8,128)S(1)}, u32[]{:S(2)}) copy-start(f32[64,64]{1,0:T(8,128)S(1)} %get-tuple-element.96) | copy-start | bytes 49156
  10.9 45.7 %copy-start.78 = (f32[192]{0:T(256)}, f32[192]{0:T(256)S(1)}, u32[]{:S(2)}) copy-start(f32[192]{0:T(256)S(1)} %neg.29) | copy-start | bytes 2308
  13.6 610.9 %copy-start.49 = (f32[2048]{0:T(1024)}, f32[2048]{0:T(1024)S(1)}, u32[]{:S(2)}) copy-start(f32[2048]{0:T(1024)S(1)} %fusion.174) | copy-start | bytes 24580
  16.0 40.6 %copy-start.74 = (f32[768]{0:T(1024)S(1)}, f32[768]{0:T(1024)}, u32[]{:S(2)}) copy-start(f32[768]{0:T(1024)} %param.21) | copy-start | bytes 9220
  16.0 40.5 %copy-start.89 = (bf16[768,3,192]{0,2,1:T(8,128)(2,1)S(1)}, bf16[768,3,192]{0,2,1:T(8,128)(2,1)}, u32[]{:S(2)}) copy-start(bf16[768,3,192]{0,2,1:T(8,128)(2,1)} %param.23) | copy-start | bytes 2654212
  16.0 40.5 %copy-start.93 = (f32[768]{0:T(1024)S(1)}, f32[768]{0:T(1024)}, u32[]{:S(2)}) copy-start(f32[768]{0:T(1024)} %param.22) | copy-start | bytes 9220
  16.0 42.9 %copy-start.45 = (f32[2048]{0:T(1024)}, f32[2048]{0:T(1024)S(1)}, u32[]{:S(2)}) copy-start(f32[2048]{0:T(1024)S(1)} %broadcast_multiply_fusion.5) | copy-start | bytes 24580
  19.0 39.8 %copy-start.60 = (f32[2048]{0:T(1024)}, f32[2048]{0:T(1024)S(1)}, u32[]{:S(2)}) copy-start(f32[2048]{0:T(1024)S(1)} %fusion.43) | copy-start | bytes 24580
  19.1 39.8 %copy-start.56 = (f32[2048]{0:T(1024)}, f32[2048]{0:T(1024)S(1)}, u32[]{:S(2)}) copy-start(f32[2048]{0:T(1024)S(1)} %fusion.175) | copy-start | bytes 24580
  19.1 39.8 %copy-start.68 = (f32[3,192]{1,0:T(4,128)}, f32[3,192]{1,0:T(4,128)S(1)}, u32[]{:S(2)}) copy-start(f32[3,192]{1,0:T(4,128)S(1)} %get-tuple-element.88) | copy-start | bytes 6916
  19.1 39.8 %copy-start.70 = (f32[3,192]{1,0:T(4,128)}, f32[3,192]{1,0:T(4,128)S(1)}, u32[]{:S(2)}) copy-start(f32[3,192]{1,0:T(4,128)S(1)} %get-tuple-element.90) | copy-start | bytes 6916
  19.1 39.8 %copy-start.72 = (f32[3,192]{1,0:T(4,128)}, f32[3,192]{1,0:T(4,128)S(1)}, u32[]{:S(2)}) copy-start(f32[3,192]{1,0:T(4,128)S(1)} %get-tuple-element.89) | copy-start | bytes 6916
  19.2 86.4 %copy-start.39 = (f32[64,64]{0,1:T(8,128)}, f32[64,64]{0,1:T(8,128)S(1)}, u32[]{:S(2)}) copy-start(f32[64,64]{0,1:T(8,128)S(1)} %copy.55) | copy-start | bytes 49156
  19.3 86.3 %copy-start.41 = (f32[64,64]{0,1:T(8,128)}, f32[64,64]{0,1:T(8,128)S(1)}, u32[]{:S(2)}) copy-start(f32[64,64]{0,1:T(8,128)S(1)} %copy.53) | copy-start | bytes 49156
  19.3 37.2 %copy-start.2 = (bf16[2048,768]{1,0:T(8,128)(2,1)S(1)}, bf16[2048,768]{1,0:T(8,128)(2,1)}, u32[]{:S(2)}) copy-start(bf16[2048,768]{1,0:T(8,128)(2,1)} %param.19) | copy-start | bytes 9437188
  322.1 10.4 copy-start.84
  329.7 7.9 copy-start.34
  336.7 73.2 %copy-start.51 = (f32[768]{0:T(1024)S(1)}, f32[768]{0:T(1024)}, u32[]{:S(2)}) copy-start(f32[768]{0:T(1024)} %param.30) | copy-start | bytes 9220
  340.3 76.2 %copy-start.66 = (f32[768]{0:T(1024)S(1)}, f32[768]{0:T(1024)}, u32[]{:S(2)}) copy-start(f32[768]{0:T(1024)} %param.31) | copy-start | bytes 9220
  340.3 76.2 %copy-start.91 = (f32[768]{0:T(1024)S(1)}, f32[768]{0:T(1024)}, u32[]{:S(2)}) copy-start(f32[768]{0:T(1024)} %param.32) | copy-start | bytes 9220
  340.3 173.6 %all-reduce.23.cloned.1.call-start = ((), (), s32[]{:S(2)}) async-start(), calls=%async_computation.2 | async-start | bytes 6291456 | tf_op jit(solution)/shard_map/psum | solution.py:247
  414.6 192.7 %copy-start.43 = (f32[2048]{0:T(1024)}, f32[2048]{0:T(1024)S(1)}, u32[]{:S(2)}) copy-start(f32[2048]{0:T(1024)S(1)} %broadcast_multiply_fusion.4) | copy-start | bytes 24580
  416.6 190.7 %copy-start.54 = (f32[2048]{0:T(1024)}, f32[2048]{0:T(1024)S(1)}, u32[]{:S(2)}) copy-start(f32[2048]{0:T(1024)S(1)} %fusion.176) | copy-start | bytes 24580
  420.5 19.1 %copy-start.28 = (f32[2048,768]{1,0:T(8,128)}, f32[2048,768]{1,0:T(8,128)S(1)}, u32[]{:S(2)}) copy-start(f32[2048,768]{1,0:T(8,128)S(1)} %fusion.278) | copy-start | bytes 18874372
  445.2 153.1 %all-gather.3.cloned.1.call-start = ((), (), s32[]{:S(2)}) async-start(), calls=%async_computation.5 | async-start | bytes 15728640 | tf_op jit(solution)/shard_map/all_gather | solution.py:10
  456.4 669.4 %all-reduce.25.cloned.1.call-start = ((), (), s32[]{:S(2)}) async-start(), calls=%async_computation.3 | async-start | bytes 6291456 | tf_op jit(solution)/shard_map/psum | solution.py:267
  598.3 9.0 copy-start.83
  607.3 10.2 copy-start.29
  654.8 25.8 %copy-start.8 = (f32[64,960,32]{1,0,2:T(8,128)S(1)}, f32[64,960,32]{1,0,2:T(8,128)}, u32[]{:S(2)}) copy-start(f32[64,960,32]{1,0,2:T(8,128)} %dot_general.142) | copy-start | bytes 23592964
  654.8 25.8 %copy-start.40 = (f32[64,64]{0,1:T(8,128)S(1)}, f32[64,64]{0,1:T(8,128)}, u32[]{:S(2)}) copy-start(f32[64,64]{0,1:T(8,128)} %copy-done.39) | copy-start | bytes 49156
  654.8 25.8 %copy-start.42 = (f32[64,64]{0,1:T(8,128)S(1)}, f32[64,64]{0,1:T(8,128)}, u32[]{:S(2)}) copy-start(f32[64,64]{0,1:T(8,128)} %copy-done.41) | copy-start | bytes 49156
  907.5 31.8 %slice-start.4 = ((s8[6291456]{0:T(1024)(128)(4,1)}), s8[4194304]{0:T(1024)(128)(4,1)S(1)}, s32[]{:S(2)}) async-start(s8[6291456]{0:T(1024)(128)(4,1)} %bitcast.170), calls=%async_computation.11 | async-start | bytes 8388608
  920.0 19.3 %slice-start.5 = ((s8[6291456]{0:T(1024)(128)(4,1)}), s8[2097152]{0:T(1024)(128)(4,1)S(1)}, s32[]{:S(2)}) async-start(s8[6291456]{0:T(1024)(128)(4,1)} %bitcast.170), calls=%async_computation.12 | async-start | bytes 4194304
  939.3 12.6 copy-start.36
  939.3 12.6 copy-start.38
  1003.9 7.7 copy-start.15
  1034.3 7.6 slice-start
  1057.2 11.5 copy-start.20
  1057.2 135.7 %reduce-scatter.2.cloned.1.call-start = ((), (), s32[]{:S(2)}) async-start(), calls=%async_computation.4 | async-start | bytes 884736 | tf_op jit(solution)/shard_map/reduce_scatter | solution.py:272
  1071.1 9.0 copy-start.24
  1073.1 11.4 copy-start.32
  1073.1 11.4 copy-start.46
  1073.1 11.4 copy-start.57
  1073.1 11.4 copy-start.75
  1073.1 11.4 copy-start.94
  1073.1 265.3 %all-reduce.27.cloned.1.call-start = ((), (), s32[]{:S(2)}) async-start(), calls=%async_computation.6 | async-start | bytes 7077888 | tf_op jit(solution)/shard_map/psum | solution.py:294
  1073.4 11.2 copy-start.4
  1090.4 41.7 %copy-start.61 = (f32[2048]{0:T(1024)S(1)}, f32[2048]{0:T(1024)}, u32[]{:S(2)}) copy-start(f32[2048]{0:T(1024)} %copy-done.60) | copy-start | bytes 24580
  1128.2 9.0 copy-start.80
  1128.2 9.0 copy-start.81
  1128.2 9.0 copy-start.86
  1128.2 9.0 copy-start.87
  1128.2 66.2 %copy-start.76 = (f32[768]{0:T(1024)S(1)}, f32[768]{0:T(1024)}, u32[]{:S(2)}) copy-start(f32[768]{0:T(1024)} %param.21) | copy-start | bytes 9220
  1194.4 152.8 %copy-start.1 = (bf16[768,768]{1,0:T(8,128)(2,1)S(1)}, bf16[768,768]{1,0:T(8,128)(2,1)}, u32[]{:S(2)}) copy-start(bf16[768,768]{1,0:T(8,128)(2,1)} %param.35) | copy-start | bytes 3538948
  1338.4 7.3 copy-start.33
  (45 other events, 172.8 us)
Sparse Core Ops, SparseCore 0:
  340.4 69.4 all-reduce.20
  445.3 68.5 all-reduce.22
  516.1 82.2 all-gather.2
  1057.3 68.4 all-reduce.24
  1129.5 63.2 reduce-scatter.1
  1198.9 139.4 all-reduce.26
